TPU v7x, 128 devices: a whole 4x4x4 slice. The times are simulated.
128 devices in a mesh: tm: 32 (over x, z, core), tp: 4 (over y).
Axes of the slice: x: 4, y: 4, z: 4, core: 2. Of those that a mesh axis runs over, the one named last changes fastest.
Arguments:
- trajectory: float32 [64, 128, 3072], P('tm', None, 'tp'), may hold values from -6 to 6
- offset: int32 [1], replicated, may hold values from 0 to 63
- step_gaps: int32 [64], P('tm'), may hold values from 1 to 4, as said below
- qkv_weight: bfloat16 [3072, 3, 3072], P(None, None, 'tp')
- out_weight: bfloat16 [3072, 3072], P('tp'), may hold values from -4 to 4
- mod_weight: bfloat16 [256, 3, 3072], P(None, None, 'tp'), may hold values from -0.375 to 0.375
Outputs:
- advanced: float32 [64, 128, 3072], P('tm', None, 'tp')
Inputs may be any that keep to these rules, and one draw needn't show every extreme that they name: `step_gaps`: in aligned blocks of 2 timesteps, the gaps of block b sum to an even number for even b and to an odd number for odd b.
All inputs are finite; a program needn't handle non-finite values.
Results may differ from a plain program's by a relative error of at most 0.007.
Values may be sent and summed in bfloat16 or wider, within the bound.
No kernel may reach another device: no remote copies, remote signals or barrier semaphores. Data moves between devices by JAX's collectives and lax.ppermute only.
A program may use at most 128 MiB of HBM per device.

v0:
```python
import math
import jax
import jax.numpy as jnp
from jax import lax
from jax.sharding import PartitionSpec as P

HD = 128
FREQ = 256
ITERS = 2


def prefix(array, axis, combine, identity):
    size, place = (lax.axis_size(axis), lax.axis_index(axis))
    everything = lax.all_gather(array, axis)
    start = jnp.broadcast_to(jnp.asarray(identity, array.dtype), array.shape)

    def turn(k, before):
        reached = k < place
        new = combine(before, everything[k])
        return jnp.where(reached, new, before)

    return lax.fori_loop(0, size, turn, start)


def broadcast(block, axis, holder):
    block = jnp.where(lax.axis_index(axis) == holder, block, jnp.zeros_like(block))
    return lax.psum(block, axis)


def prefix_2(array, axis, join, neutral):
    place = lax.axis_index(axis)
    gathered = lax.all_gather(array.astype(jnp.bfloat16), axis)
    state = jnp.zeros_like(array) + jnp.asarray(neutral, array.dtype)

    def one(turn, state):
        return join(state, lax.dynamic_index_in_dim(gathered, turn, 0, False).astype(array.dtype))

    return lax.fori_loop(0, place, one, state)


def add_up(earlier, later):
    return earlier + later


def embedding(sigma):
    half_freq = FREQ // 2
    frequencies = jnp.exp(-math.log(10000.0) * jnp.arange(half_freq, dtype=jnp.float32) / half_freq)
    angles = 1000.0 * sigma[:, None] * frequencies[None, :]
    return jnp.concatenate([jnp.cos(angles), jnp.sin(angles)], -1).astype(jnp.bfloat16)


def body(trajectory, offset, step_gaps, qkv_weight, out_weight, mod_weight):
    steps_here, tok_count, col_count = trajectory.shape
    full_width = qkv_weight.shape[0]
    time_count = steps_here * lax.axis_size("tm")
    level_count = 5 * time_count
    before = prefix(jnp.sum(step_gaps), "tm", add_up, jnp.int32(0))
    levels = (offset[0] + before + jnp.cumsum(step_gaps) - step_gaps).astype(jnp.float32)
    sigma = 1.0 - levels / level_count
    step_size = step_gaps.astype(jnp.float32) / level_count
    embed_rows = embedding(sigma)
    full_mod = lax.all_gather(mod_weight, "tp", axis=2, tiled=True)
    modulation = jnp.dot(
        embed_rows, full_mod.reshape(FREQ, 3 * full_width), preferred_element_type=jnp.float32
    ).reshape(steps_here, 3, full_width)
    gate_rows = lax.dynamic_slice_in_dim(
        modulation[:, 2], lax.axis_index("tp") * col_count, col_count, 1
    )
    base_point = broadcast(trajectory[0], "tm", 0)
    flat_qkv = qkv_weight.reshape(full_width, -1)
    states = trajectory
    points = trajectory
    for sweep in range(ITERS):
        whole_rows = lax.all_gather(states, "tp", axis=2, tiled=True)
        row_mean = jnp.sum(whole_rows, -1, keepdims=True) / full_width
        variance = (
            jnp.sum(whole_rows * whole_rows, -1, keepdims=True) / full_width - row_mean * row_mean
        )
        inv_std = lax.rsqrt(variance + 1e-06)
        normed = (
            (whole_rows - row_mean) * inv_std * (1.0 + modulation[:, 1][:, None, :])
            + modulation[:, 0][:, None, :]
        ).astype(jnp.bfloat16)
        projected = jnp.einsum("std,de->ste", normed, flat_qkv, preferred_element_type=jnp.float32)
        projected = projected.astype(jnp.bfloat16).reshape(steps_here, tok_count, 3, -1, HD)
        queries = projected[:, :, 0]
        key_rows = projected[:, :, 1]
        values = projected[:, :, 2]
        scores = jnp.einsum(
            "sqhd,skhd->shqk", queries, key_rows, preferred_element_type=jnp.float32
        ) * (1.0 / math.sqrt(HD))
        row_max = jnp.max(scores, -1, keepdims=True)
        weights_exp = jnp.exp(scores - row_max)
        probs = (weights_exp / jnp.sum(weights_exp, -1, keepdims=True)).astype(jnp.bfloat16)
        attended = jnp.einsum(
            "shqk,skhd->sqhd", probs, values, preferred_element_type=jnp.float32
        ).astype(jnp.bfloat16)
        attended = attended.reshape(steps_here, tok_count, -1)
        head_out = jnp.einsum(
            "sqe,ed->sqd", attended, out_weight, preferred_element_type=jnp.float32
        )
        col_share = lax.psum_scatter(
            head_out.astype(jnp.bfloat16), "tp", scatter_dimension=2, tiled=True
        ).astype(jnp.float32)
        drifts = gate_rows[:, None, :] * col_share
        increments = -step_size[:, None, None] * drifts
        local_cum = jnp.cumsum(increments, 0)
        prefix_sum = prefix_2(
            local_cum[-1], "tm", add_up, jnp.zeros((tok_count, col_count), jnp.float32)
        )
        entry_point = prefix_sum + base_point
        points = entry_point[None] + local_cum
        states = jnp.concatenate([entry_point[None], points[:-1]], 0)
    return points


def solution(mesh):
    placed = (
        P("tm", None, "tp"),
        P(),
        P("tm"),
        P(None, None, "tp"),
        P("tp", None),
        P(None, None, "tp"),
    )
    return jax.shard_map(
        body, mesh=mesh, in_specs=placed, out_specs=P("tm", None, "tp"), check_vma=False
    )
```

profile of v0, /device:TPU:103, one launch (start us, length us, event | category | flops | bytes accessed | tf_op | source)
XLA Modules:
  0.0 483.2 jit_solution(12489201418532556773)
XLA Ops:
  7.3 2.4 copy.33
  11.3 18.7 %copy.34 = bf16[3072,3,768]{0,2,1:T(8,128)(2,1)} copy(bf16[3072,3,768]{2,0,1:T(8,128)(2,1)} %param.15) | data formatting | bytes 28311552 | tf_op args[3]
  30.7 1.4 dynamic-update-slice
  32.0 8.7 %all-reduce = s32[32]{0:T(128)S(1)} all-reduce(s32[32]{0:T(128)S(1)} %dynamic-update-slice), channel_id=1, replica_groups=mesh['tm'=32,'tp'=4] {'tm'}, use_global_device_ids=true, to_apply=%add | all-reduce | flops 32 | bytes 256
  40.7 40.6 %while.33 = (s32[]{:T(128)}, s32[]{:T(128)}, s32[]{:T(128)}, s32[32]{0:T(128)S(1)}, s32[]{:T(128)}) while((s32[]{:T(128)}, s32[]{:T(128)}, s32[]{:T(128)}, s32[32]{0:T(128)S(1)}, s32[]{:T(128)}) %tuple.62), condition=%wide.region_2.3_spmd, body=%wide.region_1.2_spmd.sunk | while | flops 5 | bytes 107 | solution.py:22
  81.5 2.5 fusion.55
  84.0 20.4 %all-gather.6.cloned.1.call-done = bf16[256,3,3072]{0,2,1:T(8,128)(2,1)} async-done(((bf16[256,3,768]{0,2,1:T(8,128)(2,1)}), bf16[256,3,3072]{0,2,1:T(8,128)(2,1)}) %all-gather.6.cloned.1.call-update) | async-done | bytes 4718608 | tf_op jit(solution)/shard_map/all_gather | solution.py:62
  104.4 3.6 fusion.2
  108.1 10.1 %convolution_convert_fusion.1 = bf16[2,128,2304]{2,1,0:T(8,128)(2,1)} fusion(bf16[3072,2304,1]{0,1,2:T(8,128)(2,1)} %bitcast.116, f32[2,128,3072]{2,1,0:T(8,128)S(1)} %copy-done, f32[2,3072]{1,0:T(2,128)S(1)} %get-tuple-element.162, f32[2,3072]{1,0:T(2,128)S(1)} %get-tuple-element.163, f32[2,128]{1,0:T(2,128)S(1)} %get-tuple-element.167, ...), kind=kOutput, calls=%fused_computation.13 | convolution fusion | flops 3628400640 | bytes 18532352 | tf_op jit(solution)/shard_map/std,de->ste/dot_general | solution.py:84
  118.2 1.7 copy.36
  121.0 4.9 %fusion.8 = bf16[2,128,3072]{2,1,0:T(8,128)(2,1)} fusion(bf16[2,128,768]{1,2,0:T(8,128)(2,1)S(1)} %bitcast.125, bf16[768,3072]{1,0:T(8,128)(2,1)} %param.16), kind=kOutput, calls=%fused_computation.10 | convolution fusion | flops 1208745984 | bytes 6684672 | tf_op jit(solution)/shard_map/sqe,ed->sqd/dot_general | solution.py:99
  126.0 25.2 %reduce-scatter.3.cloned.1.call-done = bf16[2,128,768]{2,1,0:T(8,128)(2,1)} async-done(((bf16[2,128,3072]{2,1,0:T(8,128)(2,1)}), bf16[2,128,768]{2,1,0:T(8,128)(2,1)}) %reduce-scatter.3.cloned.1.call-update) | async-done | bytes 393232 | tf_op jit(solution)/shard_map/reduce_scatter | solution.py:102
  151.2 1.1 fusion.30
  154.0 47.3 %all-gather.10.cloned.1.call-done = bf16[32,128,768]{2,1,0:T(8,128)(2,1)} async-done(((bf16[1,128,768]{2,1,0:T(8,128)(2,1)}), bf16[32,128,768]{2,1,0:T(8,128)(2,1)}) %all-gather.10.cloned.1.call-update) | async-done | bytes 6291472 | tf_op jit(solution)/shard_map/all_gather | solution.py:32
  201.3 31.9 %while.34 = (s32[]{:T(128)}, f32[128,768]{1,0:T(8,128)S(1)}, s32[]{:T(128)}, bf16[32,128,768]{2,1,0:T(8,128)(2,1)}, s32[]{:T(128)}, /*index=5*/s32[]{:T(128)}, s32[]{:T(128)}) while((s32[]{:T(128)}, f32[128,768]{1,0:T(8,128)S(1)}, s32[]{:T(128)}, bf16[32,128,768]{2,1,0:T(8,128)(2,1)}, s32[]{:T(128)}, /*index=5*/s32[]{:T(128)}, ...), condition=%wide.region_11.12_spmd, body=%wide.region_10.11_spmd.sunk | while | flops 196613 | bytes 983155 | solution.py:38
  201.3 1.0 convert_add_fusion.4
  202.4 1.0 convert_add_fusion.4
  203.4 1.0 convert_add_fusion.4
  204.4 1.0 convert_add_fusion.4
  205.5 1.0 convert_add_fusion.4
  206.5 1.0 convert_add_fusion.4
  207.5 1.0 convert_add_fusion.4
  208.5 1.0 convert_add_fusion.4
  209.6 1.0 convert_add_fusion.4
  211.6 1.0 convert_add_fusion.4
  212.7 1.0 convert_add_fusion.4
  213.7 1.0 convert_add_fusion.4
  214.7 1.0 convert_add_fusion.4
  215.7 1.0 convert_add_fusion.4
  216.8 1.0 convert_add_fusion.4
  217.8 1.0 convert_add_fusion.4
  218.8 1.0 convert_add_fusion.4
  219.9 1.0 convert_add_fusion.4
  220.9 1.0 convert_add_fusion.4
  221.9 1.0 convert_add_fusion.4
  223.0 1.0 convert_add_fusion.4
  224.0 1.0 convert_add_fusion.4
  225.0 1.0 convert_add_fusion.4
  226.0 1.0 convert_add_fusion.4
  227.1 1.0 convert_add_fusion.4
  228.1 1.0 convert_add_fusion.4
  229.1 1.0 convert_add_fusion.4
  230.2 1.0 convert_add_fusion.4
  231.2 1.0 convert_add_fusion.4
  232.2 1.0 convert_add_fusion.4
  233.2 73.6 %all-reduce.3.cloned.1.call-done = f32[128,768]{1,0:T(8,128)} async-done(((f32[128,768]{1,0:T(8,128)}), f32[128,768]{1,0:T(8,128)}) %all-reduce.3.cloned.1.call-update) | async-done | bytes 393232 | tf_op jit(solution)/shard_map/psum | solution.py:27
  306.8 1.0 add.136
  309.1 40.2 %all-gather.12.cloned.1.call-done = f32[2,128,3072]{2,1,0:T(8,128)} async-done(((f32[2,128,768]{2,1,0:T(8,128)}), f32[2,128,3072]{2,1,0:T(8,128)}) %all-gather.12.cloned.1.call-update) | async-done | bytes 3145744 | tf_op jit(solution)/shard_map/all_gather | solution.py:74
  349.3 2.6 fusion.54
  352.1 9.1 %convolution_convert_fusion = bf16[2,128,2304]{2,1,0:T(8,128)(2,1)S(1)} fusion(bf16[3072,2304,1]{0,1,2:T(8,128)(2,1)} %bitcast.117, f32[2,128,3072]{2,1,0:T(8,128)S(1)} %copy-done.1, f32[2,128]{1,0:T(2,128)S(1)} %get-tuple-element.165, f32[2,128]{1,0:T(2,128)S(1)} %get-tuple-element.164, f32[2,3072]{1,0:T(2,128)S(1)} %get-tuple-element.162, ...), kind=kOutput, calls=%fused_computation.12 | convolution fusion | flops 3628400640 | bytes 18532352 | tf_op jit(solution)/shard_map/std,de->ste/dot_general | solution.py:84
  363.1 4.9 %fusion.11 = bf16[2,128,3072]{2,1,0:T(8,128)(2,1)} fusion(bf16[2,128,768]{1,2,0:T(8,128)(2,1)S(1)} %bitcast.126, bf16[768,3072]{1,0:T(8,128)(2,1)} %param.16), kind=kOutput, calls=%fused_computation.11 | convolution fusion | flops 1208745984 | bytes 6684672 | tf_op jit(solution)/shard_map/sqe,ed->sqd/dot_general | solution.py:99
  368.1 25.1 %reduce-scatter.5.cloned.1.call-done = bf16[2,128,768]{2,1,0:T(8,128)(2,1)} async-done(((bf16[2,128,3072]{2,1,0:T(8,128)(2,1)}), bf16[2,128,768]{2,1,0:T(8,128)(2,1)}) %reduce-scatter.5.cloned.1.call-update) | async-done | bytes 393232 | tf_op jit(solution)/shard_map/reduce_scatter | solution.py:102
  393.2 1.1 fusion.26
  395.0 48.4 %all-gather.14.cloned.1.call-done = bf16[32,128,768]{2,1,0:T(8,128)(2,1)} async-done(((bf16[1,128,768]{2,1,0:T(8,128)(2,1)}), bf16[32,128,768]{2,1,0:T(8,128)(2,1)}) %all-gather.14.cloned.1.call-update) | async-done | bytes 6291472 | tf_op jit(solution)/shard_map/all_gather | solution.py:32
  443.5 31.9 %while.35 = (s32[]{:T(128)}, f32[128,768]{1,0:T(8,128)S(1)}, s32[]{:T(128)}, bf16[32,128,768]{2,1,0:T(8,128)(2,1)}, s32[]{:T(128)}, /*index=5*/s32[]{:T(128)}, s32[]{:T(128)}) while((s32[]{:T(128)}, f32[128,768]{1,0:T(8,128)S(1)}, s32[]{:T(128)}, bf16[32,128,768]{2,1,0:T(8,128)(2,1)}, s32[]{:T(128)}, /*index=5*/s32[]{:T(128)}, ...), condition=%wide.region_20.21_spmd, body=%wide.region_19.20_spmd.sunk | while | flops 196613 | bytes 983155 | solution.py:38
  443.5 1.0 convert_add_fusion.5
  444.5 1.0 convert_add_fusion.5
  445.5 1.0 convert_add_fusion.5
  447.6 1.0 convert_add_fusion.5
  448.6 1.0 convert_add_fusion.5
  449.7 1.0 convert_add_fusion.5
  450.7 1.0 convert_add_fusion.5
  451.7 1.0 convert_add_fusion.5
  452.7 1.0 convert_add_fusion.5
  (111 shorter events, 52.9 us)
Async XLA Ops:
  6.5 3.3 copy-start.4
  6.5 75.0 %all-gather.8.cloned.1.call-start = ((), (), s32[]{:S(2)}) async-start(), calls=%async_computation.3 | async-start | bytes 3932160 | tf_op jit(solution)/shard_map/all_gather | solution.py:74
  7.3 97.2 %all-gather.6.cloned.1.call-start = ((), (), s32[]{:S(2)}) async-start(), calls=%async_computation.2 | async-start | bytes 5898240 | tf_op jit(solution)/shard_map/all_gather | solution.py:62
  9.7 141.5 %reduce-scatter.3.cloned.1.call-start = ((), (), s32[]{:S(2)}) async-start(), calls=%async_computation.4 | async-start | bytes 1966080 | tf_op jit(solution)/shard_map/reduce_scatter | solution.py:102
  11.3 18.7 %copy-start.5 = (u32[128]{0:T(128)S(1)}, u32[128]{0:T(128)}, u32[]{:S(2)}) copy-start(u32[128]{0:T(128)} %constant.91) | copy-start | bytes 1540
  84.0 24.1 %copy-start = (f32[2,128,3072]{2,1,0:T(8,128)S(1)}, f32[2,128,3072]{2,1,0:T(8,128)}, u32[]{:S(2)}) copy-start(f32[2,128,3072]{2,1,0:T(8,128)} %all-gather.8.cloned.1.call-done) | copy-start | bytes 9437188
  125.9 27.2 %copy-start.2 = (f32[2,128,768]{2,1,0:T(8,128)S(1)}, f32[2,128,768]{2,1,0:T(8,128)}, u32[]{:S(2)}) copy-start(f32[2,128,768]{2,1,0:T(8,128)} %param.12) | copy-start | bytes 2359300
  125.9 75.4 %all-gather.10.cloned.1.call-start = ((), (), s32[]{:S(2)}) async-start(), calls=%async_computation.5 | async-start | bytes 6488064 | tf_op jit(solution)/shard_map/all_gather | solution.py:32
  153.0 153.8 %all-reduce.3.cloned.1.call-start = ((), (), s32[]{:S(2)}) async-start(), calls=%async_computation.6 | async-start | bytes 786432 | tf_op jit(solution)/shard_map/psum | solution.py:27
  153.9 195.4 %all-gather.12.cloned.1.call-start = ((), (), s32[]{:S(2)}) async-start(), calls=%async_computation.7 | async-start | bytes 3932160 | tf_op jit(solution)/shard_map/all_gather | solution.py:74
  308.9 84.3 %reduce-scatter.5.cloned.1.call-start = ((), (), s32[]{:S(2)}) async-start(), calls=%async_computation.8 | async-start | bytes 1966080 | tf_op jit(solution)/shard_map/reduce_scatter | solution.py:102
  349.3 2.8 copy-start.1
  368.1 75.4 %all-gather.14.cloned.1.call-start = ((), (), s32[]{:S(2)}) async-start(), calls=%async_computation.9 | async-start | bytes 6488064 | tf_op jit(solution)/shard_map/all_gather | solution.py:32
  394.3 81.1 %copy-start.3 = (f32[128,768]{1,0:T(8,128)S(1)}, f32[128,768]{1,0:T(8,128)}, u32[]{:S(2)}) copy-start(f32[128,768]{1,0:T(8,128)} %all-reduce.3.cloned.1.call-done) | copy-start | bytes 1179652
Sparse Core Ops, SparseCore 0:
  9.0 40.7 all-gather.7
  51.5 52.8 all-gather.5
  126.0 25.1 reduce-scatter.2
  153.3 47.9 all-gather.9
  204.4 102.4 all-reduce.2
  309.0 40.2 all-gather.11
  368.2 24.9 reduce-scatter.4
  395.4 47.9 all-gather.13
where the time goes:
time: 486 us; the launch traced here: 483 us
  waiting for transfers between devices  281 us (58%)
  other arithmetic  74.2 us (15%)
  local copies, waits for them, and re-layouts  46.7 us (10%)
  matrix products  34.9 us (7%)
  loops' own time  22.8 us (5%)
  between operations  14.4 us (3%)
  blocking collectives  8.69 us (2%)
    all_gather x2, waiting for transfers between devices, prefix_2(): gathered = lax.all_gather(array.astype(jnp.bfloat16), axis)  95.7 us
    psum x1, waiting for transfers between devices, broadcast(): return lax.psum(block, axis)  73.6 us
    add x62, other arithmetic, add_up(): return earlier + later  62.1 us
    reduce_scatter x2, waiting for transfers between devices, body(): lax.psum_scatter(head_out.astype(jnp.bfloat16), 'tp', scatter_dimension=2...  50.3 us
    all_gather x2, waiting for transfers between devices, body(): whole_rows = lax.all_gather(states, 'tp', axis=2, tiled=True)  40.2 us
    unnamed x17, local copies, waits for them, and re-layouts  23.4 us
    another operation x1, loops' own time, prefix(): return lax.fori_loop(0, size, turn, start)  21.1 us
    all_gather x1, waiting for transfers between devices, body(): full_mod = lax.all_gather(mod_weight, 'tp', axis=2, tiled=True)  20.4 us
  transfers between devices with their start and end apart: 8, of which 7 were waited for; matrix products, arithmetic and copies ran while one was open for 16% of the time, Pallas kernels for 0%

commit v1 on v0

--- a/solution.py
+++ b/solution.py
@@ -59,7 +59,28 @@
     sigma = 1.0 - levels / level_count
     step_size = step_gaps.astype(jnp.float32) / level_count
     embed_rows = embedding(sigma)
-    full_mod = lax.all_gather(mod_weight, "tp", axis=2, tiled=True)
+    front, side_arr, tile_out = (
+        jax.lax.psum(1, "tp"),
+        jax.lax.axis_index("tp"),
+        mod_weight.shape[2],
+    )
+    sides = tuple((tick * front if k0 == 2 else tick for k0, tick in enumerate(mod_weight.shape)))
+    full_mod = lax.dynamic_update_slice_in_dim(
+        jnp.zeros(sides, mod_weight.dtype), mod_weight, side_arr * tile_out, axis=2
+    )
+    y = all_values = mod_weight
+    for j0 in [*range(1, front // 2 + 1)]:
+        y = jax.lax.ppermute(y, "tp", tuple(((k0, (k0 + 1) % front) for k0 in range(front))))
+        full_mod = lax.dynamic_update_slice_in_dim(
+            full_mod, y, (side_arr - j0) % front * tile_out, axis=2
+        )
+        if 2 * j0 < front:
+            all_values = jax.lax.ppermute(
+                all_values, "tp", tuple(((k0, (k0 - 1) % front) for k0 in range(front)))
+            )
+            full_mod = lax.dynamic_update_slice_in_dim(
+                full_mod, all_values, (side_arr + j0) % front * tile_out, axis=2
+            )
     modulation = jnp.dot(
         embed_rows, full_mod.reshape(FREQ, 3 * full_width), preferred_element_type=jnp.float32
     ).reshape(steps_here, 3, full_width)

time: 486 us -> 507 us (1.043)
  waiting for transfers between devices: 281 us -> 304 us
    ppermute x0 -> x3, waiting for transfers between devices: none -> 38 us  [the longest x2 38 us: body(): jax.lax.ppermute(y, 'tp', tuple(((k0, (k0 + 1) % front) for k0 in range(f...]
    all_gather x1 -> x0, waiting for transfers between devices: 20.4 us -> none  [body(): full_mod = lax.all_gather(mod_weight, 'tp', axis=2, tiled=True)]
    reduce_scatter x2, waiting for transfers between devices: 50.3 us -> 55.6 us  [body(): lax.psum_scatter(head_out.astype(jnp.bfloat16), 'tp', scatter_dimension=2...]
  transfers between devices with their start and end apart: 8 -> 10, of which waited for: 7 -> 7; matrix products, arithmetic and copies ran while one was open for 16% -> 15% of each run, Pallas kernels for 0% -> 0%
where the time goes in v1:
time: 507 us; the launch traced here: 505 us
  waiting for transfers between devices  304 us (60%)
  other arithmetic  74.3 us (15%)
  local copies, waits for them, and re-layouts  45.3 us (9%)
  matrix products  31.6 us (6%)
  loops' own time  19.9 us (4%)
  between operations  14.4 us (3%)
  blocking collectives  10.7 us (2%)
    all_gather x2, waiting for transfers between devices, prefix_2(): gathered = lax.all_gather(array.astype(jnp.bfloat16), axis)  96 us
    psum x1, waiting for transfers between devices, broadcast(): return lax.psum(block, axis)  73.6 us
    add x62, other arithmetic, add_up(): return earlier + later  62.1 us
    reduce_scatter x2, waiting for transfers between devices, body(): lax.psum_scatter(head_out.astype(jnp.bfloat16), 'tp', scatter_dimension=2...  55.6 us
    all_gather x2, waiting for transfers between devices, body(): whole_rows = lax.all_gather(states, 'tp', axis=2, tiled=True)  40.2 us
    ppermute x2, waiting for transfers between devices, body(): jax.lax.ppermute(y, 'tp', tuple(((k0, (k0 + 1) % front) for k0 in range(f...  38 us
    unnamed x17, local copies, waits for them, and re-layouts  22.7 us
    dot_general x2, matrix products, body(): jnp.einsum('std,de->ste', normed, flat_qkv, preferred_element_type=jnp.fl...  18.2 us
  transfers between devices with their start and end apart: 10, of which 7 were waited for; matrix products, arithmetic and copies ran while one was open for 15% of the time, Pallas kernels for 0%

profile of v1, /device:TPU:103, one launch (start us, length us, event | category | flops | bytes accessed | tf_op | source)
XLA Modules:
  0.0 504.7 jit_solution(6879230840672959516)
XLA Ops:
  7.3 1.6 copy.35
  8.9 1.4 collective-permute-start
  10.2 1.5 collective-permute-start.1
  11.8 38.0 %collective-permute-done = bf16[256,3,768]{0,2,1:T(8,128)(2,1)S(1)} collective-permute-done((bf16[256,3,768]{0,2,1:T(8,128)(2,1)S(1)}, bf16[256,3,768]{0,2,1:T(8,128)(2,1)S(1)}, u32[]{:S(2)}, u32[]{:S(2)}) %collective-permute-start) | collective-permute-done | bytes 1179680 | tf_op jit(solution)/shard_map/ppermute | solution.py:73
  52.1 18.7 %copy.38 = bf16[3072,3,768]{0,2,1:T(8,128)(2,1)} copy(bf16[3072,3,768]{2,0,1:T(8,128)(2,1)} %param.15) | data formatting | bytes 28311552 | tf_op args[3]
  71.5 1.3 dynamic-update-slice
  72.8 10.7 %all-reduce = s32[32]{0:T(128)S(1)} all-reduce(s32[32]{0:T(128)S(1)} %dynamic-update-slice), channel_id=1, replica_groups=mesh['tm'=32,'tp'=4] {'tm'}, use_global_device_ids=true, to_apply=%add | all-reduce | flops 32 | bytes 256
  83.5 35.9 %while.33 = (s32[]{:T(128)}, s32[]{:T(128)}, s32[]{:T(128)}, s32[32]{0:T(128)S(1)}, s32[]{:T(128)}) while((s32[]{:T(128)}, s32[]{:T(128)}, s32[]{:T(128)}, s32[32]{0:T(128)S(1)}, s32[]{:T(128)}) %tuple.62), condition=%wide.region_2.3_spmd, body=%wide.region_1.2_spmd.sunk | while | flops 5 | bytes 107 | solution.py:22
  120.2 1.4 constant_dynamic-update-slice_fusion.1
  121.7 1.3 fusion.2
  123.0 2.6 fusion.55
  125.9 9.1 %convolution_convert_fusion.1 = bf16[2,128,2304]{2,1,0:T(8,128)(2,1)S(1)} fusion(bf16[3072,2304,1]{0,1,2:T(8,128)(2,1)} %bitcast.116, f32[2,128,3072]{2,1,0:T(8,128)S(1)} %copy-done, f32[2,3072]{1,0:T(2,128)S(1)} %get-tuple-element.162, f32[2,3072]{1,0:T(2,128)S(1)} %get-tuple-element.163, f32[2,128]{1,0:T(2,128)S(1)} %get-tuple-element.167, ...), kind=kOutput, calls=%fused_computation.13 | convolution fusion | flops 3628400640 | bytes 18532352 | tf_op jit(solution)/shard_map/std,de->ste/dot_general | solution.py:105
  136.9 4.9 fusion.8
  141.8 30.6 %reduce-scatter.3.cloned.1.call-done = bf16[2,128,768]{2,1,0:T(8,128)(2,1)} async-done(((bf16[2,128,3072]{2,1,0:T(8,128)(2,1)}), bf16[2,128,768]{2,1,0:T(8,128)(2,1)}) %reduce-scatter.3.cloned.1.call-update) | async-done | bytes 393232 | tf_op jit(solution)/shard_map/reduce_scatter | solution.py:123
  172.5 1.1 fusion.30
  175.2 47.5 %all-gather.7.cloned.1.call-done = bf16[32,128,768]{2,1,0:T(8,128)(2,1)} async-done(((bf16[1,128,768]{2,1,0:T(8,128)(2,1)}), bf16[32,128,768]{2,1,0:T(8,128)(2,1)}) %all-gather.7.cloned.1.call-update) | async-done | bytes 6291472 | tf_op jit(solution)/shard_map/all_gather | solution.py:32
  222.8 31.9 %while.34 = (s32[]{:T(128)}, f32[128,768]{1,0:T(8,128)S(1)}, s32[]{:T(128)}, bf16[32,128,768]{2,1,0:T(8,128)(2,1)}, s32[]{:T(128)}, /*index=5*/s32[]{:T(128)}, s32[]{:T(128)}) while((s32[]{:T(128)}, f32[128,768]{1,0:T(8,128)S(1)}, s32[]{:T(128)}, bf16[32,128,768]{2,1,0:T(8,128)(2,1)}, s32[]{:T(128)}, /*index=5*/s32[]{:T(128)}, ...), condition=%wide.region_11.12_spmd, body=%wide.region_10.11_spmd.sunk | while | flops 196613 | bytes 983155 | solution.py:38
  222.8 1.0 convert_add_fusion.4
  223.9 1.0 convert_add_fusion.4
  224.9 1.0 convert_add_fusion.4
  225.9 1.0 convert_add_fusion.4
  227.0 1.0 convert_add_fusion.4
  228.0 1.0 convert_add_fusion.4
  229.0 1.0 convert_add_fusion.4
  230.0 1.0 convert_add_fusion.4
  231.1 1.0 convert_add_fusion.4
  232.1 1.0 convert_add_fusion.4
  233.1 1.0 convert_add_fusion.4
  234.2 1.0 convert_add_fusion.4
  235.2 1.0 convert_add_fusion.4
  236.2 1.0 convert_add_fusion.4
  237.2 1.0 convert_add_fusion.4
  238.3 1.0 convert_add_fusion.4
  240.3 1.0 convert_add_fusion.4
  241.4 1.0 convert_add_fusion.4
  242.4 1.0 convert_add_fusion.4
  243.4 1.0 convert_add_fusion.4
  244.5 1.0 convert_add_fusion.4
  245.5 1.0 convert_add_fusion.4
  246.5 1.0 convert_add_fusion.4
  247.5 1.0 convert_add_fusion.4
  248.6 1.0 convert_add_fusion.4
  249.6 1.0 convert_add_fusion.4
  250.6 1.0 convert_add_fusion.4
  251.7 1.0 convert_add_fusion.4
  252.7 1.0 convert_add_fusion.4
  253.7 1.0 convert_add_fusion.4
  254.7 73.6 %all-reduce.3.cloned.1.call-done = f32[128,768]{1,0:T(8,128)} async-done(((f32[128,768]{1,0:T(8,128)}), f32[128,768]{1,0:T(8,128)}) %all-reduce.3.cloned.1.call-update) | async-done | bytes 393232 | tf_op jit(solution)/shard_map/psum | solution.py:27
  328.3 1.0 add.168
  330.6 40.2 %all-gather.9.cloned.1.call-done = f32[2,128,3072]{2,1,0:T(8,128)} async-done(((f32[2,128,768]{2,1,0:T(8,128)}), f32[2,128,3072]{2,1,0:T(8,128)}) %all-gather.9.cloned.1.call-update) | async-done | bytes 3145744 | tf_op jit(solution)/shard_map/all_gather | solution.py:95
  370.8 2.6 fusion.54
  373.6 9.1 %convolution_convert_fusion = bf16[2,128,2304]{2,1,0:T(8,128)(2,1)S(1)} fusion(bf16[3072,2304,1]{0,1,2:T(8,128)(2,1)} %bitcast.117, f32[2,128,3072]{2,1,0:T(8,128)S(1)} %copy-done.1, f32[2,128]{1,0:T(2,128)S(1)} %get-tuple-element.165, f32[2,128]{1,0:T(2,128)S(1)} %get-tuple-element.164, f32[2,3072]{1,0:T(2,128)S(1)} %get-tuple-element.162, ...), kind=kOutput, calls=%fused_computation.12 | convolution fusion | flops 3628400640 | bytes 18532352 | tf_op jit(solution)/shard_map/std,de->ste/dot_general | solution.py:105
  384.6 4.9 fusion.11
  389.6 25.0 %reduce-scatter.5.cloned.1.call-done = bf16[2,128,768]{2,1,0:T(8,128)(2,1)} async-done(((bf16[2,128,3072]{2,1,0:T(8,128)(2,1)}), bf16[2,128,768]{2,1,0:T(8,128)(2,1)}) %reduce-scatter.5.cloned.1.call-update) | async-done | bytes 393232 | tf_op jit(solution)/shard_map/reduce_scatter | solution.py:123
  414.6 1.1 fusion.26
  416.5 48.5 %all-gather.11.cloned.1.call-done = bf16[32,128,768]{2,1,0:T(8,128)(2,1)} async-done(((bf16[1,128,768]{2,1,0:T(8,128)(2,1)}), bf16[32,128,768]{2,1,0:T(8,128)(2,1)}) %all-gather.11.cloned.1.call-update) | async-done | bytes 6291472 | tf_op jit(solution)/shard_map/all_gather | solution.py:32
  465.0 31.9 %while.35 = (s32[]{:T(128)}, f32[128,768]{1,0:T(8,128)S(1)}, s32[]{:T(128)}, bf16[32,128,768]{2,1,0:T(8,128)(2,1)}, s32[]{:T(128)}, /*index=5*/s32[]{:T(128)}, s32[]{:T(128)}) while((s32[]{:T(128)}, f32[128,768]{1,0:T(8,128)S(1)}, s32[]{:T(128)}, bf16[32,128,768]{2,1,0:T(8,128)(2,1)}, s32[]{:T(128)}, /*index=5*/s32[]{:T(128)}, ...), condition=%wide.region_20.21_spmd, body=%wide.region_19.20_spmd.sunk | while | flops 196613 | bytes 983155 | solution.py:38
  465.0 1.0 convert_add_fusion.5
  466.0 1.0 convert_add_fusion.5
  467.1 1.0 convert_add_fusion.5
  468.1 1.0 convert_add_fusion.5
  469.1 1.0 convert_add_fusion.5
  470.1 1.0 convert_add_fusion.5
  471.2 1.0 convert_add_fusion.5
  (119 shorter events, 55.5 us)
Async XLA Ops:
  6.5 44.2 %copy-start.4 = (s32[2]{0:T(128)S(1)}, s32[2]{0:T(128)}, u32[]{:S(2)}) copy-start(s32[2]{0:T(128)} %param.14) | copy-start | bytes 28
  6.5 116.5 %all-gather.5.cloned.1.call-start = ((), (), s32[]{:S(2)}) async-start(), calls=%async_computation.2 | async-start | bytes 3932160 | tf_op jit(solution)/shard_map/all_gather | solution.py:95
  7.3 165.2 %reduce-scatter.3.cloned.1.call-start = ((), (), s32[]{:S(2)}) async-start(), calls=%async_computation.3 | async-start | bytes 1966080 | tf_op jit(solution)/shard_map/reduce_scatter | solution.py:123
  8.9 40.9 %collective-permute-start = (bf16[256,3,768]{0,2,1:T(8,128)(2,1)S(1)}, bf16[256,3,768]{0,2,1:T(8,128)(2,1)S(1)}, u32[]{:S(2)}, u32[]{:S(2)}) collective-permute-start(bf16[256,3,768]{0,2,1:T(8,128)(2,1)S(1)} %copy.35), channel_id=1, source_target_pairs={{0,1},{1,2},{2,3},{3,0},{4,5},{5,6},{6,7},{7,4},{8,9},{9,10},{10,1... | collective-permute-start | bytes 3538952 | tf_op jit(solution)/shard_map/ppermute | solution.py:73
  10.2 109.9 %collective-permute-start.1 = (bf16[256,3,768]{0,2,1:T(8,128)(2,1)S(1)}, bf16[256,3,768]{0,2,1:T(8,128)(2,1)}, u32[]{:S(2)}, u32[]{:S(2)}) collective-permute-start(bf16[256,3,768]{0,2,1:T(8,128)(2,1)S(1)} %copy.35), channel_id=1, source_target_pairs={{0,3},{1,0},{2,1},{3,2},{4,7},{5,4},{6,5},{7,6},{8,11},{9,8},{10,9... | collective-permute-start | bytes 3538952 | tf_op jit(solution)/shard_map/ppermute | solution.py:78
  49.8 71.7 %collective-permute-start.2 = (bf16[256,3,768]{0,2,1:T(8,128)(2,1)S(1)}, bf16[256,3,768]{0,2,1:T(8,128)(2,1)S(1)}, u32[]{:S(2)}, u32[]{:S(2)}) collective-permute-start(bf16[256,3,768]{0,2,1:T(8,128)(2,1)S(1)} %collective-permute-done), channel_id=1, source_target_pairs={{0,1},{1,2},{2,3},{3,0},{4,5},{5,6},{6,7},{7,4},{8,9},{9,10},{10,1... | collective-permute-start | bytes 3538952 | tf_op jit(solution)/shard_map/ppermute | solution.py:73
  52.1 18.7 %copy-start.5 = (u32[128]{0:T(128)S(1)}, u32[128]{0:T(128)}, u32[]{:S(2)}) copy-start(u32[128]{0:T(128)} %constant.120) | copy-start | bytes 1540
  123.0 2.8 copy-start
  141.8 32.6 %copy-start.2 = (f32[2,128,768]{2,1,0:T(8,128)S(1)}, f32[2,128,768]{2,1,0:T(8,128)}, u32[]{:S(2)}) copy-start(f32[2,128,768]{2,1,0:T(8,128)} %param.12) | copy-start | bytes 2359300
  141.8 81.0 %all-gather.7.cloned.1.call-start = ((), (), s32[]{:S(2)}) async-start(), calls=%async_computation.4 | async-start | bytes 6488064 | tf_op jit(solution)/shard_map/all_gather | solution.py:32
  174.3 154.0 %all-reduce.3.cloned.1.call-start = ((), (), s32[]{:S(2)}) async-start(), calls=%async_computation.5 | async-start | bytes 786432 | tf_op jit(solution)/shard_map/psum | solution.py:27
  175.2 195.6 %all-gather.9.cloned.1.call-start = ((), (), s32[]{:S(2)}) async-start(), calls=%async_computation.6 | async-start | bytes 3932160 | tf_op jit(solution)/shard_map/all_gather | solution.py:95
  330.4 84.2 %reduce-scatter.5.cloned.1.call-start = ((), (), s32[]{:S(2)}) async-start(), calls=%async_computation.7 | async-start | bytes 1966080 | tf_op jit(solution)/shard_map/reduce_scatter | solution.py:123
  370.8 2.8 copy-start.1
  389.6 75.4 %all-gather.11.cloned.1.call-start = ((), (), s32[]{:S(2)}) async-start(), calls=%async_computation.8 | async-start | bytes 6488064 | tf_op jit(solution)/shard_map/all_gather | solution.py:32
  415.7 81.1 %copy-start.3 = (f32[128,768]{1,0:T(8,128)S(1)}, f32[128,768]{1,0:T(8,128)}, u32[]{:S(2)}) copy-start(f32[128,768]{1,0:T(8,128)} %all-reduce.3.cloned.1.call-done) | copy-start | bytes 1179652
Sparse Core Ops, SparseCore 0:
  9.0 63.2 all-gather.4
  141.9 30.5 reduce-scatter.2
  174.8 47.9 all-gather.6
  225.9 102.4 all-reduce.2
  330.5 40.2 all-gather.8
  389.7 24.8 reduce-scatter.4
  416.9 48.0 all-gather.10
